TPU v7x, 32 devices: a whole 2x2x4 slice. The times are simulated.
32 devices in a mesh: sph: 8 (over z, x), ang: 4 (over y, core).
Axes of the slice: x: 2, y: 2, z: 4, core: 2. Of those that a mesh axis runs over, the one named last changes fastest.
Arguments:
- coefficients: bfloat16 [256, 240, 1024], P(('sph', 'ang')), may hold values from -0.039794922 to 0.039794922
- positions: int32 [256, 3], P(('sph', 'ang')), may hold values from 0 to 7
- shift_tables: bfloat16 [3, 8, 480, 240], replicated, may hold values from -1.3 to 1.3
- absorb_weight: float32 [256, 240], P(('sph', 'ang')), may hold values from 0.02 to 0.9, as said below
- incident: float32 [240, 1024], replicated, may hold values from -1.6 to 1.6
- detector: float32 [32, 64], P('sph'), may hold values from 0.002 to 0.18, as said below
Outputs:
- amplitude: float32 [2, 2, 32, 64, 512], P(None, None, 'sph', 'ang')
- cross_sections: float32 [3, 512], P(None, 'ang')
Inputs may be any that keep to these rules, and one draw needn't show every extreme that they name: `absorb_weight`: Positive. `detector`: Positive.
All inputs are finite; a program needn't handle non-finite values.
Results may differ from a plain program's by a relative error of at most 0.0003.
The roundings to bfloat16 on the way count: a program that leaves them out, or rounds other values in their place, can miss the bound.
Values sent between devices are 32-bit elements; how exact they have to be, the bound alone decides.
A program may use at most 128 MiB of HBM per device.

v0:
```python
import math

import jax
import jax.numpy as jnp
from jax import lax
from jax.sharding import PartitionSpec as P

ORDER = 10
AZIM = 64
POL_DEV = 4


def legendre_table(cos_theta, sine_theta, order):
    values = {}
    values[0, 0] = jnp.zeros_like(cos_theta) + 1.0 / math.sqrt(4.0 * math.pi)
    for azim_order in range(order + 1):
        if azim_order > 0:
            factor = -math.sqrt((2.0 * azim_order + 1.0) / (2.0 * azim_order))
            values[azim_order, azim_order] = (
                factor * sine_theta * values[azim_order - 1, azim_order - 1]
            )
        if azim_order + 1 <= order:
            values[azim_order + 1, azim_order] = (
                math.sqrt(2.0 * azim_order + 3.0) * cos_theta * values[azim_order, azim_order]
            )
        for degree in range(azim_order + 2, order + 1):
            upper_coef = math.sqrt(
                (4.0 * degree * degree - 1.0) / (degree * degree - azim_order * azim_order)
            )
            lower_coef = math.sqrt(
                ((degree - 1.0) * (degree - 1.0) - azim_order * azim_order)
                / (4.0 * (degree - 1.0) * (degree - 1.0) - 1.0)
            )
            values[degree, azim_order] = upper_coef * (
                cos_theta * values[degree - 1, azim_order]
                - lower_coef * values[degree - 2, azim_order]
            )
    return values


def angular_basis(polar_index, azim_index, polar_total, azim_total, order):
    theta = (polar_index.astype(jnp.float32) + 0.5) * (math.pi / polar_total)
    azimuth = azim_index.astype(jnp.float32) * (2.0 * math.pi / azim_total)
    cos_theta = jnp.cos(theta)
    sine_theta = jnp.sin(theta)
    legendre_values = legendre_table(cos_theta, sine_theta, order)
    pi_terms = []
    tau_terms = []
    orders_list = []
    phase_real = []
    phase_imag = []
    unit_powers = [(1.0, 0.0), (0.0, -1.0), (-1.0, 0.0), (0.0, 1.0)]
    for degree in range(1, order + 1):
        norm_factor = 1.0 / math.sqrt(degree * (degree + 1.0))
        power_real, power_imag = unit_powers[(degree + 1) % 4]
        for azim_order in range(-degree, degree + 1):
            size_m = abs(azim_order)
            current = legendre_values[degree, size_m]
            if degree - 1 >= size_m:
                previous = legendre_values[degree - 1, size_m]
            else:
                previous = jnp.zeros_like(current)
            link = math.sqrt(
                (2.0 * degree + 1.0)
                * (degree * degree - azim_order * azim_order)
                / (2.0 * degree - 1.0)
            )
            pi_terms.append(azim_order * current / sine_theta)
            tau_terms.append((degree * cos_theta * current - link * previous) / sine_theta)
            orders_list.append(float(azim_order))
            phase_real.append(power_real * norm_factor)
            phase_imag.append(power_imag * norm_factor)
    pi_block = jnp.stack(pi_terms, axis=1)[:, None, :]
    tau_block = jnp.stack(tau_terms, axis=1)[:, None, :]
    orders_row = jnp.array(orders_list, dtype=jnp.float32)
    angle_table = azimuth[:, None] * orders_row[None, :]
    cos_table = jnp.cos(angle_table)
    sin_table = jnp.sin(angle_table)
    scale_real = jnp.array(phase_real, dtype=jnp.float32)[None, :]
    scale_imag = jnp.array(phase_imag, dtype=jnp.float32)[None, :]
    wave_real = (scale_real * cos_table - scale_imag * sin_table)[None, :, :]
    wave_imag = (scale_real * sin_table + scale_imag * cos_table)[None, :, :]
    theta_real = jnp.concatenate([-pi_block * wave_imag, tau_block * wave_real], axis=-1)
    theta_imag = jnp.concatenate([pi_block * wave_real, tau_block * wave_imag], axis=-1)
    phi_real = jnp.concatenate([-tau_block * wave_real, -pi_block * wave_imag], axis=-1)
    phi_imag = jnp.concatenate([-tau_block * wave_imag, pi_block * wave_real], axis=-1)
    real_part = jnp.stack([theta_real, phi_real])
    imag_part = jnp.stack([theta_imag, phi_imag])
    return (real_part, imag_part, sine_theta)


def evaluate_far(real_part, imag_part, anchor):
    half = anchor.shape[1] // 2
    first = jnp.einsum("cikp,pf->cikf", real_part, anchor, precision=lax.Precision.HIGHEST)
    second = jnp.einsum("cikp,pf->cikf", imag_part, anchor, precision=lax.Precision.HIGHEST)
    real_out = first[..., :half] - second[..., half:]
    imag_out = first[..., half:] + second[..., :half]
    return jnp.stack([real_out, imag_out], axis=1)


def rotate_step(matrix, vector):
    product = jnp.einsum("sap,spf->saf", matrix, vector, preferred_element_type=jnp.float32)
    half_rows = matrix.shape[2]
    half_cols = vector.shape[2] // 2
    real_out = product[:, :half_rows, :half_cols] - product[:, half_rows:, half_cols:]
    imag_out = product[:, half_rows:, :half_cols] + product[:, :half_rows, half_cols:]
    return jnp.concatenate([real_out, imag_out], axis=2)


def shards(coefficients, positions, shift_tables, absorb_weight, incident, detector):
    fields = coefficients.shape[2] // 2
    coef_count = coefficients.shape[1]
    along_z = jnp.take(shift_tables[2], positions[:, 2], axis=0)
    along_y = jnp.take(shift_tables[1], positions[:, 1], axis=0)
    along_x = jnp.take(shift_tables[0], positions[:, 0], axis=0)
    first = rotate_step(along_z, coefficients).astype(jnp.bfloat16)
    second = rotate_step(along_y, first).astype(jnp.bfloat16)
    moved = rotate_step(along_x, second)
    partial_value = jnp.sum(moved, axis=0)
    widened = coefficients.astype(jnp.float32)
    squares = widened * widened
    energy = squares[:, :, :fields] + squares[:, :, fields:]
    absorbed = jnp.einsum("sp,spf->f", absorb_weight, energy)
    extinction = jnp.sum(
        incident[:, :fields] * partial_value[:, :fields]
        + incident[:, fields:] * partial_value[:, fields:],
        axis=0,
    )
    local_stats = jnp.stack([extinction, absorbed])
    partial_split = partial_value.reshape(coef_count, 2, fields)
    polar_total = POL_DEV * lax.axis_size("sph")
    polar_index = lax.axis_index("sph") * POL_DEV + jnp.arange(POL_DEV)
    groups = lax.axis_size("ang")
    share = fields // groups
    solid_angle = 2.0 * math.pi * math.pi / (polar_total * AZIM)
    anchor_split, stats = lax.psum((partial_split, local_stats), ("sph", "ang"))
    azim_share = AZIM // groups
    azim_start = lax.axis_index("ang") * azim_share
    azim_index = azim_start + jnp.arange(azim_share)
    real_part, imag_part, sine_theta = angular_basis(
        polar_index, azim_index, polar_total, AZIM, ORDER
    )
    amplitude = evaluate_far(real_part, imag_part, anchor_split.reshape(coef_count, 2 * fields))
    local_detector = lax.dynamic_slice_in_dim(detector, azim_start, azim_share, 1)
    weight = local_detector * sine_theta[:, None] * solid_angle
    power = jnp.einsum("crikf,ik->f", amplitude * amplitude, weight)
    collected = lax.psum_scatter(power, "ang", scatter_dimension=0, tiled=True)
    collected = lax.psum(collected, "sph")
    own_stats = lax.dynamic_slice_in_dim(stats, lax.axis_index("ang") * share, share, 1)
    cross_sections = jnp.concatenate([own_stats, collected[None, :]], axis=0)
    return (amplitude, cross_sections)


def solution(mesh):
    placed = (
        P(("sph", "ang"), None, None),
        P(("sph", "ang"), None),
        P(),
        P(("sph", "ang"), None),
        P(),
        P("sph", None),
    )
    return jax.shard_map(
        shards,
        mesh=mesh,
        in_specs=placed,
        out_specs=(P(None, None, "sph", "ang", None), P(None, "ang")),
        check_vma=False,
    )
```

profile of v0, /device:TPU:0, one launch (start us, length us, event | category | flops | bytes accessed | tf_op | source)
XLA Modules:
  0.0 254.2 jit_solution(17758391303258946681)
XLA Ops:
  7.2 5.3 %slice_bitcast_fusion.2 = (bf16[8,480,240]{2,1,0:T(8,128)(2,1)}, bf16[8,480,240]{2,1,0:T(8,128)(2,1)}, bf16[8,480,240]{2,1,0:T(8,128)(2,1)}) fusion(bf16[3,8,480,240]{3,2,1,0:T(8,128)(2,1)} %param.13), kind=kLoop, calls=%fused_computation.32 | loop fusion | bytes 11059200 | tf_op jit(solution)/shard_map/squeeze | solution.py:115
  12.6 2.2 gather_fusion.2
  14.8 9.8 %fusion.14 = f32[8,480,1024]{2,1,0:T(8,128)} fusion(bf16[8,240,1024]{2,1,0:T(8,128)(2,1)} %param.11, bf16[8,480,240]{2,1,0:T(8,128)(2,1)S(1)} %gather_fusion.2, pred[8]{0:T(512)(128)(4,1)S(1)} %get-tuple-element.41), kind=kOutput, calls=%fused_computation.26 | convolution fusion | flops 1888358400 | bytes 21504008 | tf_op jit(solution)/shard_map/sap,spf->saf/dot_general | solution.py:102
  24.6 9.0 %fusion.5 = (bf16[8,240,512]{2,1,0:T(8,128)(2,1)}, bf16[8,240,512]{2,1,0:T(8,128)(2,1)}) fusion(f32[8,480,1024]{2,1,0:T(8,128)} %fusion.14), kind=kLoop, calls=%fused_computation.17 | loop fusion | flops 3932160 | bytes 19660800 | tf_op jit(solution)/shard_map/convert.2
  33.6 2.2 gather_fusion.1
  35.9 9.8 %fusion.6 = f32[8,480,1024]{2,1,0:T(8,128)} fusion(bf16[8,240,512]{2,1,0:T(8,128)(2,1)} %get-tuple-element.18, bf16[8,240,512]{2,1,0:T(8,128)(2,1)} %get-tuple-element.17, bf16[8,480,240]{2,1,0:T(8,128)(2,1)S(1)} %gather_fusion.1, pred[8]{0:T(512)(128)(4,1)S(1)} %get-tuple-element.43), kind=kOutput, calls=%fused_computation.18 | convolution fusion | flops 1896222720 | bytes 21504008 | tf_op jit(solution)/shard_map/sap,spf->saf/dot_general | solution.py:102
  45.7 9.1 %fusion.3 = (bf16[8,240,512]{2,1,0:T(8,128)(2,1)}, bf16[8,240,512]{2,1,0:T(8,128)(2,1)}) fusion(f32[8,480,1024]{2,1,0:T(8,128)} %fusion.6), kind=kLoop, calls=%fused_computation.13 | loop fusion | flops 3932160 | bytes 19660800 | tf_op jit(solution)/shard_map/convert
  54.8 2.2 gather_fusion
  57.0 9.8 %fusion.10 = f32[8,480,1024]{2,1,0:T(8,128)} fusion(bf16[8,240,512]{2,1,0:T(8,128)(2,1)} %get-tuple-element.16, bf16[8,240,512]{2,1,0:T(8,128)(2,1)} %get-tuple-element.15, bf16[8,480,240]{2,1,0:T(8,128)(2,1)S(1)} %gather_fusion, pred[8]{0:T(512)(128)(4,1)S(1)} %get-tuple-element.7), kind=kOutput, calls=%fused_computation.22 | convolution fusion | flops 1896222720 | bytes 21504008 | tf_op jit(solution)/shard_map/sap,spf->saf/dot_general | solution.py:102
  66.8 7.8 %slice_subtract_fusion = (f32[8,240,512]{2,1,0:T(8,128)S(1)}, f32[8,240,512]{2,1,0:T(8,128)S(1)}) fusion(f32[8,480,1024]{2,1,0:T(8,128)} %fusion.10), kind=kLoop, calls=%fused_computation.9 | loop fusion | flops 1966080 | bytes 23592960 | tf_op jit(solution)/shard_map/sub | solution.py:105
  74.6 0.9 maximum_reduce_fusion
  76.1 0.4 copy-done.1
  76.5 0.3 all-reduce.3.cloned.1.call-update
  82.9 6.4 %convert_multiply_fusion = f32[8,240,1024]{2,1,0:T(8,128)} fusion(bf16[8,240,1024]{2,1,0:T(8,128)(2,1)} %param.11), kind=kLoop, calls=%fused_computation.4 | loop fusion | flops 3932160 | bytes 11796480 | tf_op jit(solution)/shard_map/mul | solution.py:121
  89.9 3.8 %fusion.21 = f32[1,512]{1,0:T(1,128)S(1)} fusion(f32[8,240,1024]{2,1,0:T(8,128)} %convert_multiply_fusion, f32[8,240,1]{1,0,2:T(8,128)S(1)} %bitcast.50), kind=kOutput, calls=%fused_computation.36 | convolution fusion | flops 2949120 | bytes 7874048 | tf_op jit(solution)/shard_map/sp,spf->f/dot_general | solution.py:123
  93.7 42.0 %psum.22 = f32[2,512]{1,0:T(2,128)S(1)} all-reduce(f32[2,512]{1,0:T(2,128)S(1)} %pad_maximum_fusion.1), channel_id=1, replica_groups=mesh['sph'=8,'ang'=4] {'sph','ang'}, use_global_device_ids=true, to_apply=%region_3.5 | all-reduce | flops 1024 | bytes 8192 | tf_op jit(solution)/shard_map/psum | solution.py:136
  135.9 0.6 dynamic-slice
  137.4 76.9 %all-reduce.3.cloned.1.call-done = f32[240,1024]{1,0:T(8,128)} async-done(((f32[240,1024]{1,0:T(8,128)}), f32[240,1024]{1,0:T(8,128)}) %all-reduce.3.cloned.1.call-update) | async-done | bytes 983056 | tf_op jit(solution)/shard_map/psum | solution.py:136
  214.3 1.9 fusion.22
  216.2 1.9 fusion.24
  218.2 0.8 copy.12
  219.3 6.8 %all-reduce = f32[512]{0:T(512)S(1)} all-reduce(f32[512]{0:T(512)S(1)} %bitcast.53), channel_id=2, replica_groups=mesh['sph'=8,'ang'=4] {'ang'}, use_global_device_ids=true, to_apply=%region_5.7.clone | all-reduce | flops 512 | bytes 4096
  226.2 20.6 %psum.23 = f32[1,128]{1,0:T(1,128)S(1)} all-reduce(f32[1,128]{1,0:T(1,128)S(1)} %dynamic-slice_bitcast_fusion), channel_id=1, replica_groups=mesh['sph'=8,'ang'=4] {'sph'}, use_global_device_ids=true, to_apply=%region_6.8 | all-reduce | flops 128 | bytes 1024 | tf_op jit(solution)/shard_map/psum | solution.py:148
  246.8 0.6 pad_maximum_fusion.2
  (132 shorter events, 7.8 us)
Async XLA Ops:
  7.2 82.7 %copy-start = (f32[8,240]{1,0:T(8,128)S(1)}, f32[8,240]{1,0:T(8,128)}, u32[]{:S(2)}) copy-start(f32[8,240]{1,0:T(8,128)} %param.14) | copy-start | bytes 23044
  7.2 5.4 %copy-start.4 = (s32[8,3]{0,1:T(4,128)S(1)}, s32[8,3]{0,1:T(4,128)}, u32[]{:S(2)}) copy-start(s32[8,3]{0,1:T(4,128)} %param.12) | copy-start | bytes 292
  74.6 1.2 copy-start.2
  75.5 0.9 copy-start.1
  76.0 138.2 %all-reduce.3.cloned.1.call-start = ((), (), s32[]{:S(2)}) async-start(), calls=%async_computation | async-start | bytes 1966080 | tf_op jit(solution)/shard_map/psum | solution.py:136
  89.3 46.3 %copy-start.5 = (f32[120]{0:T(128)S(1)}, f32[120]{0:T(128)}, u32[]{:S(2)}) copy-start(f32[120]{0:T(128)} %constant.609.clone) | copy-start | bytes 1444
  89.3 46.3 %copy-start.6 = (f32[120]{0:T(128)S(1)}, f32[120]{0:T(128)}, u32[]{:S(2)}) copy-start(f32[120]{0:T(128)} %constant.607.clone) | copy-start | bytes 1444
  89.3 46.3 %copy-start.7 = (f32[120]{0:T(128)S(1)}, f32[120]{0:T(128)}, u32[]{:S(2)}) copy-start(f32[120]{0:T(128)} %constant.608.clone) | copy-start | bytes 1444
  89.3 46.5 %copy-start.8 = (u32[32]{0:T(128)S(1)}, u32[32]{0:T(128)}, u32[]{:S(2)}) copy-start(u32[32]{0:T(128)} %constant.616) | copy-start | bytes 388
  89.3 48.0 %copy-start.3 = (f32[4,64]{1,0:T(4,128)S(1)}, f32[4,64]{1,0:T(4,128)}, u32[]{:S(2)}) copy-start(f32[4,64]{1,0:T(4,128)} %param.16) | copy-start | bytes 3076
Sparse Core Ops, SparseCore 0:
  82.0 132.1 all-reduce.2
where the time goes:
time: 255 us; the launch traced here: 254 us
  waiting for transfers between devices  77.1 us (30%)
  blocking collectives  69.4 us (27%)
  other arithmetic  40.4 us (16%)
  matrix products  37.2 us (15%)
  between operations  15.3 us (6%)
  local copies, waits for them, and re-layouts  14.7 us (6%)
    psum x1, waiting for transfers between devices, shards(): anchor_split, stats = lax.psum((partial_split, local_stats), ('sph', 'ang'))  76.9 us
    psum x1, blocking collectives, shards(): anchor_split, stats = lax.psum((partial_split, local_stats), ('sph', 'ang'))  42 us
    dot_general x3, matrix products, rotate_step(): jnp.einsum('sap,spf->saf', matrix, vector, preferred_element_type=jnp.flo...  29.4 us
    psum x1, blocking collectives, shards(): collected = lax.psum(collected, 'sph')  20.6 us
    another operation x2, other arithmetic  18.1 us
    sub x1, other arithmetic, rotate_step(): product[:, :half_rows, :half_cols] - product[:, half_rows:, half_cols:]  7.76 us
    unnamed x1, blocking collectives  6.84 us
    mul x1, other arithmetic, shards(): squares = widened * widened  6.4 us
  transfers between devices with their start and end apart: 1, of which 1 were waited for; matrix products, arithmetic and copies ran while one was open for 7% of the time, Pallas kernels for 0%

commit v1 on v0

v1 whole, which is shorter than its diff:
```python
import functools
import math

import jax
import jax.numpy as jnp
import numpy as np
from jax import lax
from jax.experimental import pallas as pl
from jax.experimental.pallas import tpu as pltpu
from jax.sharding import PartitionSpec as P

MESH = pl.DeviceIdType.MESH


def angular_tables(polar_total, azim_total, order):
    theta = (np.arange(polar_total) + 0.5) * (math.pi / polar_total)
    azimuth = np.arange(azim_total) * (2.0 * math.pi / azim_total)
    cos_theta, sine = np.cos(theta), np.sin(theta)
    leg = {(0, 0): np.full_like(theta, 1.0 / math.sqrt(4.0 * math.pi))}
    for m in range(order + 1):
        if m > 0:
            leg[m, m] = -math.sqrt((2.0 * m + 1.0) / (2.0 * m)) * sine * leg[m - 1, m - 1]
        if m + 1 <= order:
            leg[m + 1, m] = math.sqrt(2.0 * m + 3.0) * cos_theta * leg[m, m]
        for n in range(m + 2, order + 1):
            upper = math.sqrt((4.0 * n * n - 1.0) / (n * n - m * m))
            lower = math.sqrt(((n - 1.0) ** 2 - m * m) / (4.0 * (n - 1.0) ** 2 - 1.0))
            leg[n, m] = upper * (cos_theta * leg[n - 1, m] - lower * leg[n - 2, m])
    pis, taus, waves = [], [], []
    for n in range(1, order + 1):
        for m in range(-n, n + 1):
            s = abs(m)
            prev = leg[n - 1, s] if n - 1 >= s else np.zeros_like(theta)
            link = math.sqrt((2.0 * n + 1.0) * (n * n - m * m) / (2.0 * n - 1.0))
            pis.append(m * leg[n, s] / sine)
            taus.append((n * cos_theta * leg[n, s] - link * prev) / sine)
            unit = (1.0, -1j, -1.0, 1j)[(n + 1) % 4]
            waves.append(unit * np.exp(1j * m * azimuth) / math.sqrt(n * (n + 1.0)))
    pi, tau, wave = np.stack(pis, 1), np.stack(taus, 1), np.stack(waves, 1)
    wr, wi = wave.real, wave.imag
    polar = np.stack([np.concatenate([pi, tau] * 2, 1), np.concatenate([tau, pi] * 2, 1)])
    azim = np.stack([
        np.concatenate([-wi, wr, -wr, -wi], 1),
        np.concatenate([wr, wi, -wi, wr], 1),
        np.concatenate([-wr, -wi, wi, -wr], 1),
        np.concatenate([-wi, wr, -wr, -wi], 1),
    ])
    return polar, azim, sine


def rotate(table, real, imag):
    half = table.shape[0] // 2
    width = real.shape[1]
    product = jnp.dot(table, jnp.concatenate([real, imag], 1), preferred_element_type=jnp.float32)
    return (
        product[:half, :width] - product[half:, width:],
        product[half:, :width] + product[:half, width:],
    )


def local_kernel(chunks, pos_ref, c_ref, z_ref, y_ref, x_ref, aw_ref, out_ref):
    j = pl.program_id(0)
    coef = c_ref.shape[1]
    fields = c_ref.shape[2] // 2
    width = fields // chunks

    @pl.when(j == 0)
    def _():
        out_ref[...] = jnp.zeros_like(out_ref)

    lane = lax.broadcasted_iota(jnp.int32, aw_ref.shape, 1)
    column = jnp.sum(jnp.where(lane == j, aw_ref[...], 0.0), axis=1, keepdims=True)
    for h in range(chunks):
        cols = slice(h * width, (h + 1) * width)
        vr = c_ref[0, :, cols]
        vi = c_ref[0, :, slice(fields + h * width, fields + (h + 1) * width)]
        fr, fi = rotate(z_ref[0, 0], vr, vi)
        fr, fi = rotate(y_ref[0, 0], fr.astype(jnp.bfloat16), fi.astype(jnp.bfloat16))
        fr, fi = rotate(x_ref[0, 0], fr.astype(jnp.bfloat16), fi.astype(jnp.bfloat16))
        out_ref[:coef, cols] += fr
        out_ref[coef : 2 * coef, cols] += fi
        wr, wi = vr.astype(jnp.float32), vi.astype(jnp.float32)
        energy = (wr * wr + wi * wi) * column
        out_ref[2 * coef : 2 * coef + 1, cols] += jnp.sum(energy, axis=0, keepdims=True)


def local_part(coefficients, positions, shift_tables, absorb_weight, rows):
    spheres, coef, columns = coefficients.shape
    fields = columns // 2

    def table(axis):
        return pl.BlockSpec((1, 1, 2 * coef, coef), lambda j, pos: (axis, pos[j, axis], 0, 0))

    return pl.pallas_call(
        functools.partial(local_kernel, 2),
        grid_spec=pltpu.PrefetchScalarGridSpec(
            num_scalar_prefetch=1,
            grid=(spheres,),
            in_specs=[
                pl.BlockSpec((1, coef, columns), lambda j, pos: (j, 0, 0)),
                table(2),
                table(1),
                table(0),
                pl.BlockSpec((coef, spheres), lambda j, pos: (0, 0)),
            ],
            out_specs=pl.BlockSpec((rows, fields), lambda j, pos: (0, 0)),
        ),
        out_shape=jax.ShapeDtypeStruct((rows, fields), jnp.float32),
        compiler_params=pltpu.CompilerParams(dimension_semantics=("arbitrary",)),
    )(positions, coefficients, shift_tables, shift_tables, shift_tables, absorb_weight.T)


def split(value):
    high = value.astype(jnp.bfloat16)
    return high, (value - high.astype(jnp.float32)).astype(jnp.bfloat16)


def far_kernel(
    sph_n, ang_n, coef, pol,
    part, det, inc_hbm, pol_hbm, azi_hbm, amp_hbm, stats,
    h_in, acc, recv1, gath, inc, tpol, tazi, basis, amp, pow_send, pow_recv,
    s0, r0, s1, r1, s2, r2, s3, r3, s4, r4, lsem,
):
    n = sph_n * ang_n
    pairs = ang_n // 2
    m = n // 2
    sph, ang = lax.axis_index("sph"), lax.axis_index("ang")
    p = lax.rem(ang, 2)
    chip = sph * pairs + ang // 2
    me = sph * ang_n + ang
    partner = (sph, ang + 1 - 2 * p)

    def peer(c):
        return (c // pairs, 2 * lax.rem(c, pairs) + p)

    def device(d):
        return (d // ang_n, lax.rem(d, ang_n))

    local = [
        pltpu.make_async_copy(inc_hbm, inc, lsem.at[0]),
        pltpu.make_async_copy(pol_hbm.at[sph], tpol, lsem.at[1]),
        pltpu.make_async_copy(azi_hbm.at[ang], tazi, lsem.at[2]),
    ]
    for copy in local:
        copy.start()

    barrier = pltpu.get_barrier_semaphore()

    def greet(k, carry):
        pl.semaphore_signal(
            barrier, inc=1, device_id=device(lax.rem(me + k, n)), device_id_type=MESH
        )
        return carry

    lax.fori_loop(1, n, greet, 0)
    pl.semaphore_wait(barrier, n - 1)

    def copy0(c):
        return pltpu.make_async_remote_copy(
            part.at[(1 - p) * m + c], h_in.at[c], s0.at[c], r0.at[c], partner, MESH
        )

    def copy1(c, slot):
        return pltpu.make_async_remote_copy(
            acc.at[c], recv1.at[slot], s1.at[c], r1.at[slot], peer(c), MESH
        )

    def copy2(c, slot):
        row = gath.at[p * m + slot]
        return pltpu.make_async_remote_copy(row, row, s2.at[c], r2.at[slot], peer(c), MESH)

    def copy3(c, half):
        row = gath.at[half * m + c]
        return pltpu.make_async_remote_copy(row, row, s3.at[c], r3.at[c], partner, MESH)

    def copy4(d, slot):
        return pltpu.make_async_remote_copy(
            pow_send, pow_recv.at[slot], s4.at[d], r4.at[slot], device(d), MESH
        )

    def loop(low, high, body):
        def step(k, carry):
            body(k)
            return carry

        lax.fori_loop(low, high, step, 0)

    loop(1, m + 1, lambda k: copy0(lax.rem(chip + k, m)).start())

    def first(c):
        copy0(c).wait_recv()
        acc[c] = part[p * m + c] + h_in[c]

    def exchange(k):
        c = lax.rem(chip + k, m)
        first(c)
        copy1(c, chip).start()

    loop(1, m, exchange)
    first(chip)

    for copy in local:
        copy.wait()
    azi = tazi.shape[1]
    block = pol * azi
    for cr in range(4):
        for i in range(pol):
            basis[cr * block + i * azi : cr * block + (i + 1) * azi, :] = (
                tpol[cr // 2, i : i + 1, :] * tazi[cr]
            )

    def gather_sum(k, total):
        c = lax.rem(chip - k + m, m)
        copy1(c, c).wait_recv()
        return total + recv1[c]

    gath[p * m + chip] = lax.fori_loop(1, m, gather_sum, acc[chip])
    copy3(chip, p).start()
    loop(1, m, lambda k: copy2(lax.rem(chip + k, m), chip).start())

    def forward(k):
        c = lax.rem(chip - k + m, m)
        copy2(c, c).wait_recv()
        copy3(c, p).start()

    loop(1, m, forward)
    loop(0, m, lambda k: copy3(k, 1 - p).wait_recv())

    rows = gath.shape[0] * gath.shape[1]
    fields = gath.shape[2]
    anchor = gath[...].reshape(rows, fields)
    a_high, a_low = split(anchor[: 2 * coef])
    w_high, w_low = split(basis[:, : 2 * coef])
    dot = functools.partial(jnp.dot, preferred_element_type=jnp.float32)
    far = dot(w_high, a_high) + (dot(w_high, a_low) + dot(w_low, a_high))
    amp[...] = far
    out_copy = pltpu.make_async_copy(amp, amp_hbm, lsem.at[0])
    out_copy.start()

    azim_total = det.shape[1]
    want = lax.broadcasted_iota(jnp.int32, (azi, azim_total), 0) + ang * azi
    lane = lax.broadcasted_iota(jnp.int32, (azi, azim_total), 1)
    power = jnp.zeros((1, fields), jnp.float32)
    for i in range(pol):
        weight = jnp.sum(
            jnp.where(lane == want, det[i : i + 1, :], 0.0), axis=1, keepdims=True
        ) * tpol[0, i : i + 1, 2 * coef : 2 * coef + 1]
        total = jnp.zeros((azi, fields), jnp.float32)
        for cr in range(4):
            piece = far[cr * block + i * azi : cr * block + (i + 1) * azi, :]
            total = total + piece * piece
        power = power + jnp.sum(total * weight, axis=0, keepdims=True)
    pow_send[...] = power
    pow_recv[me] = power
    loop(1, n, lambda k: copy4(lax.rem(me + k, n), me).start())

    stats[0:1, :] = jnp.sum(
        inc[:, :fields] * anchor[:coef] + inc[:, fields:] * anchor[coef : 2 * coef],
        axis=0, keepdims=True,
    )
    stats[1:2, :] = anchor[2 * coef : 2 * coef + 1]

    def finish(k):
        copy0(k).wait_send()
        copy3(k, p).wait_send()

    loop(0, m, finish)

    def finish_peers(k):
        c = lax.rem(chip + k, m)
        copy1(c, chip).wait_send()
        copy2(c, chip).wait_send()

    loop(1, m, finish_peers)

    def finish_power(k):
        d = lax.rem(me + k, n)
        copy4(d, d).wait_recv()
        copy4(d, me).wait_send()

    loop(1, n, finish_power)
    stats[2:3, :] = lax.fori_loop(
        1, n, lambda k, total: total + pow_recv[k], pow_recv[0]
    )
    out_copy.wait()


def far_part(part, detector, incident, polar, azim, sph_n, ang_n):
    n, r, fields = part.shape
    m = n // 2
    coef = incident.shape[0]
    pol = detector.shape[0]
    azi = azim.shape[2]
    wide = polar.shape[3]
    vmem = pl.BlockSpec(memory_space=pltpu.VMEM)
    hbm = pl.BlockSpec(memory_space=pl.ANY)
    f32 = jnp.float32
    dma = pltpu.SemaphoreType.DMA
    return pl.pallas_call(
        functools.partial(far_kernel, sph_n, ang_n, coef, pol),
        out_shape=(
            jax.ShapeDtypeStruct((4 * pol * azi, fields), f32),
            jax.ShapeDtypeStruct((3, fields), f32),
        ),
        in_specs=[vmem, vmem, hbm, hbm, hbm],
        out_specs=(hbm, vmem),
        scratch_shapes=[
            pltpu.VMEM((m, r, fields), f32),
            pltpu.VMEM((m, r, fields), f32),
            pltpu.VMEM((m, r, fields), f32),
            pltpu.VMEM((n, r, fields), f32),
            pltpu.VMEM(incident.shape, f32),
            pltpu.VMEM((2, pol, wide), f32),
            pltpu.VMEM((4, azi, wide), f32),
            pltpu.VMEM((4 * pol * azi, wide), f32),
            pltpu.VMEM((4 * pol * azi, fields), f32),
            pltpu.VMEM((1, fields), f32),
            pltpu.VMEM((n, 1, fields), f32),
        ]
        + [dma((m,))] * 8
        + [dma((n,))] * 2
        + [dma((3,))],
        compiler_params=pltpu.CompilerParams(
            collective_id=0, has_side_effects=True, vmem_limit_bytes=48 * 2**20
        ),
    )(part, detector, incident, polar, azim)


def shards(sph_n, ang_n, coefficients, positions, shift_tables, absorb_weight, incident, detector):
    fields = coefficients.shape[2] // 2
    coef = coefficients.shape[1]
    n = sph_n * ang_n
    chunk = 8 * -(-(2 * coef + 1) // (8 * n))
    pol, azim_total = detector.shape
    polar_total = pol * sph_n
    azi = azim_total // ang_n
    order = math.isqrt(coef // 2 + 1) - 1
    wide = 128 * -(-(2 * coef + 1) // 128)
    polar, azim, sine = angular_tables(polar_total, azim_total, order)
    table_polar = np.zeros((sph_n, 2, pol, wide), np.float32)
    table_polar[..., : 2 * coef] = polar.reshape(2, sph_n, pol, 2 * coef).transpose(1, 0, 2, 3)
    solid = 2.0 * math.pi * math.pi / (polar_total * azim_total)
    table_polar[..., 2 * coef] = (sine * solid).reshape(sph_n, 1, pol)
    table_azim = np.zeros((ang_n, 4, azi, wide), np.float32)
    table_azim[..., : 2 * coef] = azim.reshape(4, ang_n, azi, 2 * coef).transpose(1, 0, 2, 3)

    part = local_part(coefficients, positions, shift_tables, absorb_weight, n * chunk)
    amplitude, stats = far_part(
        part.reshape(n, chunk, fields), detector, incident,
        jnp.asarray(table_polar), jnp.asarray(table_azim), sph_n, ang_n,
    )
    share = fields // ang_n
    own = lax.dynamic_slice_in_dim(stats, lax.axis_index("ang") * share, share, 1)
    return (amplitude.reshape(2, 2, pol, azi, fields), own)


def solution(mesh):
    placed = (
        P(("sph", "ang"), None, None),
        P(("sph", "ang"), None),
        P(),
        P(("sph", "ang"), None),
        P(),
        P("sph", None),
    )
    return jax.shard_map(
        functools.partial(shards, mesh.shape["sph"], mesh.shape["ang"]),
        mesh=mesh,
        in_specs=placed,
        out_specs=(P(None, None, "sph", "ang", None), P(None, "ang")),
        check_vma=False,
    )
```

time: 255 us -> 70 us (0.27)
  waiting for transfers between devices: 77.1 us -> 0 us
  blocking collectives: 69.4 us -> 0 us
  Pallas kernels: 0 us -> 63.6 us
  other arithmetic: 40.4 us -> 0 us
  matrix products: 37.2 us -> 0 us
  between operations: 15.3 us -> 0.68 us
  local copies, waits for them, and re-layouts: 14.7 us -> 5.43 us
    psum x1 -> x0, waiting for transfers between devices: 76.9 us -> none  [shards(): anchor_split, stats = lax.psum((partial_split, local_stats), ('sph', 'ang'))]
    pallas_call x0 -> x2, Pallas kernels: none -> 63.6 us  [the longest x1 45.4 us: far_part(): pl.pallas_call(functools.partial(far_kernel, sph_n, ang_n, coef, pol), ou...]
    psum x2 -> x0, blocking collectives: 62.5 us -> none  [the longest x1 42 us: shards(): anchor_split, stats = lax.psum((partial_split, local_stats), ('sph', 'ang'))]
    dot_general x7 -> x0, matrix products: 37.2 us -> none  [the longest x3 29.4 us: rotate_step(): jnp.einsum('sap,spf->saf', matrix, vector, preferred_element_type=jnp.flo...]
    another operation x6 -> x0, other arithmetic: 18.4 us -> none
    sub x1 -> x0, other arithmetic: 7.76 us -> none  [rotate_step(): product[:, :half_rows, :half_cols] - product[:, half_rows:, half_cols:]]
    unnamed x1 -> x0, blocking collectives: 6.84 us -> none
    gather x3 -> x0, local copies, waits for them, and re-layouts: 6.65 us -> none  [the longest x1 2.22 us: shards(): along_z = jnp.take(shift_tables[2], positions[:, 2], axis=0)]
  transfers between devices with their start and end apart: 1 -> 0, of which waited for: 1 -> 0; matrix products, arithmetic and copies ran while one was open for 7% -> 0% of each run, Pallas kernels for 0% -> 0%
where the time goes in v1:
time: 70 us; the launch traced here: 69.7 us
  Pallas kernels  63.6 us (91%)
  local copies, waits for them, and re-layouts  5.43 us (8%)
    pallas_call x1, Pallas kernels, far_part(): pl.pallas_call(functools.partial(far_kernel, sph_n, ang_n, coef, pol), ou...  45.4 us
    pallas_call x1, Pallas kernels, local_part(): pl.pallas_call(functools.partial(local_kernel, 2), grid_spec=pltpu.Prefet...  18.2 us
    unnamed x13, local copies, waits for them, and re-layouts  4.84 us

profile of v1, /device:TPU:0, one launch (start us, length us, event | category | flops | bytes accessed | tf_op | source)
XLA Modules:
  0.0 69.7 jit_solution(11036872649083484480)
XLA Ops:
  0.6 1.3 %copy.11.pos_ref = s32[8,3]{1,0:T(8,128)} copy(s32[8,3]{0,1:T(4,128)} %param.9) | data formatting | bytes 192 | tf_op args[1]
  2.0 1.5 %copy.10 = f32[8,240]{0,1:T(8,128)} copy(f32[8,240]{1,0:T(8,128)} %param.11) | data formatting | bytes 15360 | tf_op args[3]
  3.4 0.0 copy-start.1
  3.5 0.0 copy-start.2
  3.5 0.0 copy-start.3
  3.5 0.0 copy-start.4
  3.5 18.2 %shard_map.95 = f32[512,512]{1,0:T(8,128)} custom-call(s32[8,3]{1,0:T(8,128)} %copy.11.pos_ref, bf16[8,240,1024]{2,1,0:T(8,128)(2,1)} %c_ref.1, bf16[3,8,480,240]{3,2,1,0:T(8,128)(2,1)} %x_ref.1, bf16[3,8,480,240]{3,2,1,0:T(8,128)(2,1)} %x_ref.1, bf16[3,8,480,240]{3,2,1,0:T(8,128)(2,1)} %x_ref.1, f32[240,8]{1,0:T(8,128)} %bitcast.5), custom_call_target="tpu_custom_call" | custom-call | tf_op jit(solution)/shard_map/pallas_call | solution.py:94
  21.7 0.0 copy-done.1
  21.7 0.0 copy-done.2
  21.7 0.0 copy-done.3
  21.7 0.0 copy-done.4
  21.7 0.0 copy-start
  21.7 1.2 %copy-done = f32[512,512]{1,0:T(8,128)S(1)} copy-done((f32[512,512]{1,0:T(8,128)S(1)}, f32[512,512]{1,0:T(8,128)}, u32[]{:S(2)}) %copy-start) | copy-done | bytes 1048600
  22.9 45.4 %shard_map.96 = (f32[256,512]{1,0:T(8,128)S(1)}, f32[3,512]{1,0:T(4,128)S(1)}) custom-call(f32[32,16,512]{2,1,0:T(8,128)S(1)} %bitcast.3, f32[4,64]{1,0:T(4,128)S(1)} %copy-done.4, f32[240,1024]{1,0:T(8,128)S(1)} %copy-done.1, f32[8,2,4,512]{3,2,1,0:T(4,128)S(1)} %copy-done.3, f32[4,4,16,512]{3,2,1,0:T(8,128)S(1)} %copy-done.2), custom_call_target="tpu_custom_call" | custom-call | tf_op jit(solution)/shard_map/pallas_call | solution.py:299
  68.4 0.6 constant_dynamic-slice_fusion
  69.0 0.8 %copy.13 = f32[2,2,4,16,512]{4,3,2,1,0:T(8,128)} copy(f32[2,2,4,16,512]{4,3,2,1,0:T(8,128)S(1)} %bitcast.4) | data formatting | bytes 1048576
Async XLA Ops:
  3.4 18.2 %copy-start.1 = (f32[240,1024]{1,0:T(8,128)S(1)}, f32[240,1024]{1,0:T(8,128)}, u32[]{:S(2)}) copy-start(f32[240,1024]{1,0:T(8,128)} %inc_hbm.1) | copy-start | bytes 2949124
  3.5 18.2 %copy-start.2 = (f32[4,4,16,512]{3,2,1,0:T(8,128)S(1)}, f32[4,4,16,512]{3,2,1,0:T(8,128)}, u32[]{:S(2)}) copy-start(f32[4,4,16,512]{3,2,1,0:T(8,128)} %constant.15.clone.azi_hbm) | copy-start | bytes 1572868
  3.5 18.2 %copy-start.3 = (f32[8,2,4,512]{3,2,1,0:T(4,128)S(1)}, f32[8,2,4,512]{3,2,1,0:T(4,128)}, u32[]{:S(2)}) copy-start(f32[8,2,4,512]{3,2,1,0:T(4,128)} %constant.14.clone.pol_hbm) | copy-start | bytes 393220
  3.5 18.3 %copy-start.4 = (f32[4,64]{1,0:T(4,128)S(1)}, f32[4,64]{1,0:T(4,128)}, u32[]{:S(2)}) copy-start(f32[4,64]{1,0:T(4,128)} %det.1) | copy-start | bytes 3076
  21.7 1.2 %copy-start = (f32[512,512]{1,0:T(8,128)S(1)}, f32[512,512]{1,0:T(8,128)}, u32[]{:S(2)}) copy-start(f32[512,512]{1,0:T(8,128)} %shard_map.95) | copy-start | bytes 3145732

commit v2 on v1

--- a/solution.py
+++ b/solution.py
@@ -68,8 +68,9 @@
     def _():
         out_ref[...] = jnp.zeros_like(out_ref)
 
-    lane = lax.broadcasted_iota(jnp.int32, aw_ref.shape, 1)
-    column = jnp.sum(jnp.where(lane == j, aw_ref[...], 0.0), axis=1, keepdims=True)
+    weight = aw_ref[...].T
+    lane = lax.broadcasted_iota(jnp.int32, weight.shape, 1)
+    column = jnp.sum(jnp.where(lane == j, weight, 0.0), axis=1, keepdims=True)
     for h in range(chunks):
         cols = slice(h * width, (h + 1) * width)
         vr = c_ref[0, :, cols]
@@ -89,10 +90,10 @@
     fields = columns // 2
 
     def table(axis):
-        return pl.BlockSpec((1, 1, 2 * coef, coef), lambda j, pos: (axis, pos[j, axis], 0, 0))
+        return pl.BlockSpec((1, 1, 2 * coef, coef), lambda j, pos: (axis, pos[axis, j], 0, 0))
 
     return pl.pallas_call(
-        functools.partial(local_kernel, 2),
+        functools.partial(local_kernel, 1),
         grid_spec=pltpu.PrefetchScalarGridSpec(
             num_scalar_prefetch=1,
             grid=(spheres,),
@@ -101,13 +102,13 @@
                 table(2),
                 table(1),
                 table(0),
-                pl.BlockSpec((coef, spheres), lambda j, pos: (0, 0)),
+                pl.BlockSpec((spheres, coef), lambda j, pos: (0, 0)),
             ],
-            out_specs=pl.BlockSpec((rows, fields), lambda j, pos: (0, 0)),
+            out_specs=pl.BlockSpec(memory_space=pltpu.VMEM),
         ),
         out_shape=jax.ShapeDtypeStruct((rows, fields), jnp.float32),
         compiler_params=pltpu.CompilerParams(dimension_semantics=("arbitrary",)),
-    )(positions, coefficients, shift_tables, shift_tables, shift_tables, absorb_weight.T)
+    )(positions.T, coefficients, shift_tables, shift_tables, shift_tables, absorb_weight)
 
 
 def split(value):
@@ -118,20 +119,29 @@
 def far_kernel(
     sph_n, ang_n, coef, pol,
     part, det, inc_hbm, pol_hbm, azi_hbm, amp_hbm, stats,
-    h_in, acc, recv1, gath, inc, tpol, tazi, basis, amp, pow_send, pow_recv,
-    s0, r0, s1, r1, s2, r2, s3, r3, s4, r4, lsem,
+    h_in, acc, in_a, in_b, in_z, gath, inc, tpol, tazi, basis, amp, pow_send, pow_recv,
+    s0, r0, sa, ra, sb, rb, sz, rz, ga, gb, gz, rg, s3, r3, s4, r4, lsem,
 ):
     n = sph_n * ang_n
-    pairs = ang_n // 2
+    q = ang_n // 2
+    nz = sph_n // q
     m = n // 2
     sph, ang = lax.axis_index("sph"), lax.axis_index("ang")
     p = lax.rem(ang, 2)
-    chip = sph * pairs + ang // 2
+    x, y, z = lax.rem(sph, q), ang // 2, sph // q
+    a = x * (1 - p) + y * p
+    b = y * (1 - p) + x * p
+    chip = (a * q + b) * nz + z
     me = sph * ang_n + ang
     partner = (sph, ang + 1 - 2 * p)
 
-    def peer(c):
-        return (c // pairs, 2 * lax.rem(c, pairs) + p)
+    def peer(a2, b2, z2):
+        x2 = a2 * (1 - p) + b2 * p
+        y2 = b2 * (1 - p) + a2 * p
+        return (z2 * q + x2, 2 * y2 + p)
+
+    def at(a2, b2, z2):
+        return (a2 * q + b2) * nz + z2
 
     def device(d):
         return (d // ang_n, lax.rem(d, ang_n))
@@ -155,23 +165,47 @@
     lax.fori_loop(1, n, greet, 0)
     pl.semaphore_wait(barrier, n - 1)
 
+    remote = pltpu.make_async_remote_copy
+
     def copy0(c):
-        return pltpu.make_async_remote_copy(
-            part.at[(1 - p) * m + c], h_in.at[c], s0.at[c], r0.at[c], partner, MESH
+        return remote(part.at[(1 - p) * m + c], h_in.at[c], s0.at[c], r0.at[c], partner, MESH)
+
+    def send_a(a2, i, src):
+        return remote(
+            acc.at[a2 * q * nz + i], in_a.at[src * q * nz + i],
+            sa.at[a2 * q * nz + i], ra.at[src * q * nz + i], peer(a2, b, z), MESH,
         )
 
-    def copy1(c, slot):
-        return pltpu.make_async_remote_copy(
-            acc.at[c], recv1.at[slot], s1.at[c], r1.at[slot], peer(c), MESH
+    def send_b(b2, z2, src):
+        return remote(
+            acc.at[at(a, b2, z2)], in_b.at[src * nz + z2],
+            sb.at[b2 * nz + z2], rb.at[src * nz + z2], peer(a, b2, z), MESH,
         )
 
-    def copy2(c, slot):
-        row = gath.at[p * m + slot]
-        return pltpu.make_async_remote_copy(row, row, s2.at[c], r2.at[slot], peer(c), MESH)
+    def send_z(z2, src):
+        return remote(
+            acc.at[at(a, b, z2)], in_z.at[src], sz.at[z2], rz.at[src], peer(a, b, z2), MESH
+        )
+
+    def spread(c, send, device_id):
+        row = gath.at[p * m + c]
+        return remote(row, row, send, rg.at[c], device_id, MESH)
+
+    def spread_a(a2, b2, z2):
+        return spread(at(a, b2, z2), ga.at[at(a2, b2, z2)], peer(a2, b, z))
+
+    def spread_b(b2, z2):
+        return spread(at(a, b, z2), gb.at[b2 * nz + z2], peer(a, b2, z))
+
+    def spread_z(z2):
+        return spread(chip, gz.at[z2], peer(a, b, z2))
+
+    def arrived(c):
+        spread(c, gz.at[0], partner).wait_recv()
 
     def copy3(c, half):
         row = gath.at[half * m + c]
-        return pltpu.make_async_remote_copy(row, row, s3.at[c], r3.at[c], partner, MESH)
+        return remote(row, row, s3.at[c], r3.at[c], partner, MESH)
 
     def copy4(d, slot):
         return pltpu.make_async_remote_copy(
@@ -185,19 +219,61 @@
 
         lax.fori_loop(low, high, step, 0)
 
-    loop(1, m + 1, lambda k: copy0(lax.rem(chip + k, m)).start())
+    def shift(base, k, size):
+        return lax.rem(base + k, size)
+
+    loop(1, m + 1, lambda k: copy0(shift(b * q * nz + q * nz - 1, k, m)).start())
 
     def first(c):
         copy0(c).wait_recv()
         acc[c] = part[p * m + c] + h_in[c]
 
-    def exchange(k):
-        c = lax.rem(chip + k, m)
+    for da in range(1, q):
+        a2 = shift(a, da, q)
+
+        def step_a(k):
+            i = shift((b + 1) * nz, k, q * nz)
+            first(a2 * q * nz + i)
+            send_a(a2, i, a).start()
+
+        loop(0, q * nz, step_a)
+
+    def add_a(b2, z2):
+        c = at(a, b2, z2)
         first(c)
-        copy1(c, chip).start()
-
-    loop(1, m, exchange)
-    first(chip)
+        value = acc[c]
+        for da in range(1, q):
+            src = shift(a, da, q)
+            send_a(src, b2 * nz + z2, src).wait_recv()
+            value = value + in_a[at(src, b2, z2)]
+        acc[c] = value
+
+    for db in range(1, q):
+        b2 = shift(b, db, q)
+
+        def step_b(k):
+            z2 = shift(z, k, nz)
+            add_a(b2, z2)
+            send_b(b2, z2, b).start()
+
+        loop(1, nz + 1, step_b)
+
+    def add_b(z2):
+        add_a(b, z2)
+        value = acc[at(a, b, z2)]
+        for db in range(1, q):
+            src = shift(b, db, q)
+            send_b(src, z2, src).wait_recv()
+            value = value + in_b[src * nz + z2]
+        acc[at(a, b, z2)] = value
+
+    def step_z(k):
+        z2 = shift(z, k, nz)
+        add_b(z2)
+        send_z(z2, z).start()
+
+    loop(1, nz, step_z)
+    add_b(z)
 
     for copy in local:
         copy.wait()
@@ -210,20 +286,49 @@
             )
 
     def gather_sum(k, total):
-        c = lax.rem(chip - k + m, m)
-        copy1(c, c).wait_recv()
-        return total + recv1[c]
-
-    gath[p * m + chip] = lax.fori_loop(1, m, gather_sum, acc[chip])
-    copy3(chip, p).start()
-    loop(1, m, lambda k: copy2(lax.rem(chip + k, m), chip).start())
-
-    def forward(k):
-        c = lax.rem(chip - k + m, m)
-        copy2(c, c).wait_recv()
-        copy3(c, p).start()
-
-    loop(1, m, forward)
+        src = shift(z, k, nz)
+        send_z(src, src).wait_recv()
+        return total + in_z[src]
+
+    gath[p * m + chip] = lax.fori_loop(1, nz, gather_sum, acc[chip])
+    loop(1, nz, lambda k: spread_z(shift(z, k, nz)).start())
+
+    def plane(k):
+        z2 = shift(z, k, nz)
+        if_own = at(a, b, z2)
+        for db in range(1, q):
+            spread_b(shift(b, db, q), z2).start()
+        for da in range(1, q):
+            spread_a(shift(a, da, q), b, z2).start()
+        copy3(if_own, p).start()
+
+    plane(0)
+
+    def step_plane(k):
+        arrived(at(a, b, shift(z, k, nz)))
+        plane(k)
+
+    loop(1, nz, step_plane)
+
+    def step_line(k):
+        z2 = shift(z, k, nz)
+        for db in range(1, q):
+            b2 = shift(b, db, q)
+            arrived(at(a, b2, z2))
+            for da in range(1, q):
+                spread_a(shift(a, da, q), b2, z2).start()
+            copy3(at(a, b2, z2), p).start()
+
+    loop(0, nz, step_line)
+
+    def step_rest(k):
+        for db in range(q):
+            for da in range(1, q):
+                c = at(shift(a, da, q), shift(b, db, q), shift(z, k, nz))
+                arrived(c)
+                copy3(c, p).start()
+
+    loop(0, nz, step_rest)
     loop(0, m, lambda k: copy3(k, 1 - p).wait_recv())
 
     rows = gath.shape[0] * gath.shape[1]
@@ -266,12 +371,25 @@
 
     loop(0, m, finish)
 
-    def finish_peers(k):
-        c = lax.rem(chip + k, m)
-        copy1(c, chip).wait_send()
-        copy2(c, chip).wait_send()
-
-    loop(1, m, finish_peers)
+    def finish_plane(k):
+        for db in range(q):
+            b2 = shift(b, db, q)
+            for da in range(1, q):
+                a2 = shift(a, da, q)
+                send_a(a2, b2 * nz + k, a).wait_send()
+                spread_a(a2, b2, k).wait_send()
+            if db > 0:
+                send_b(b2, k, b).wait_send()
+                spread_b(b2, k).wait_send()
+
+    loop(0, nz, finish_plane)
+
+    def finish_line(k):
+        z2 = shift(z, k, nz)
+        send_z(z2, z).wait_send()
+        spread_z(z2).wait_send()
+
+    loop(1, nz, finish_line)
 
     def finish_power(k):
         d = lax.rem(me + k, n)
@@ -288,6 +406,8 @@
 def far_part(part, detector, incident, polar, azim, sph_n, ang_n):
     n, r, fields = part.shape
     m = n // 2
+    nz = sph_n // (ang_n // 2)
+    line = n // ang_n
     coef = incident.shape[0]
     pol = detector.shape[0]
     azi = azim.shape[2]
@@ -308,6 +428,8 @@
             pltpu.VMEM((m, r, fields), f32),
             pltpu.VMEM((m, r, fields), f32),
             pltpu.VMEM((m, r, fields), f32),
+            pltpu.VMEM((line, r, fields), f32),
+            pltpu.VMEM((nz, r, fields), f32),
             pltpu.VMEM((n, r, fields), f32),
             pltpu.VMEM(incident.shape, f32),
             pltpu.VMEM((2, pol, wide), f32),
@@ -317,7 +439,7 @@
             pltpu.VMEM((1, fields), f32),
             pltpu.VMEM((n, 1, fields), f32),
         ]
-        + [dma((m,))] * 8
+        + [dma((size,)) for size in (m, m, m, m, line, line, nz, nz, m, line, nz, m, m, m)]
         + [dma((n,))] * 2
         + [dma((3,))],
         compiler_params=pltpu.CompilerParams(

time: 70 us -> 54.8 us (0.78)
  Pallas kernels: 63.6 us -> 51.2 us
  local copies, waits for them, and re-layouts: 5.43 us -> 2.62 us
    pallas_call x1, Pallas kernels: 45.4 us -> 37.9 us  [far_part(): pl.pallas_call(functools.partial(far_kernel, sph_n, ang_n, coef, pol), ou...]
    pallas_call x1, Pallas kernels: 18.2 us -> 13.2 us  [local_part(): pl.pallas_call(functools.partial(local_kernel, 1), grid_spec=pltpu.Prefet...]
    unnamed x13 -> x11, local copies, waits for them, and re-layouts: 4.84 us -> 2.03 us
where the time goes in v2:
time: 54.8 us; the launch traced here: 54.5 us
  Pallas kernels  51.2 us (93%)
  local copies, waits for them, and re-layouts  2.62 us (5%)
  between operations  0.7 us (1%)
    pallas_call x1, Pallas kernels, far_part(): pl.pallas_call(functools.partial(far_kernel, sph_n, ang_n, coef, pol), ou...  37.9 us
    pallas_call x1, Pallas kernels, local_part(): pl.pallas_call(functools.partial(local_kernel, 1), grid_spec=pltpu.Prefet...  13.2 us
    unnamed x11, local copies, waits for them, and re-layouts  2.03 us

profile of v2, /device:TPU:0, one launch (start us, length us, event | category | flops | bytes accessed | tf_op | source)
XLA Modules:
  0.0 54.5 jit_solution(15369495031090737180)
XLA Ops:
  0.6 0.0 copy-start.1
  0.6 0.0 copy-start.2
  0.7 0.0 copy-start.3
  0.7 0.0 copy-start.4
  0.7 13.2 %shard_map.95 = f32[512,512]{1,0:T(8,128)} custom-call(s32[3,8]{1,0:T(4,128)} %bitcast.5, bf16[8,240,1024]{2,1,0:T(8,128)(2,1)} %c_ref.1, bf16[3,8,480,240]{3,2,1,0:T(8,128)(2,1)} %x_ref.1, bf16[3,8,480,240]{3,2,1,0:T(8,128)(2,1)} %x_ref.1, bf16[3,8,480,240]{3,2,1,0:T(8,128)(2,1)} %x_ref.1, f32[8,240]{1,0:T(8,128)} %aw_ref.1), custom_call_target="tpu_custom_call" | custom-call | tf_op jit(solution)/shard_map/pallas_call | solution.py:95
  13.9 0.0 copy-done.1
  13.9 0.0 copy-done.2
  13.9 0.0 copy-done.3
  13.9 0.0 copy-done.4
  13.9 0.0 copy-start
  14.0 1.2 %copy-done = f32[512,512]{1,0:T(8,128)S(1)} copy-done((f32[512,512]{1,0:T(8,128)S(1)}, f32[512,512]{1,0:T(8,128)}, u32[]{:S(2)}) %copy-start) | copy-done | bytes 1048600
  15.2 37.9 %shard_map.96 = (f32[256,512]{1,0:T(8,128)S(1)}, f32[3,512]{1,0:T(4,128)S(1)}) custom-call(f32[32,16,512]{2,1,0:T(8,128)S(1)} %bitcast.3, f32[4,64]{1,0:T(4,128)S(1)} %copy-done.4, f32[240,1024]{1,0:T(8,128)S(1)} %copy-done.1, f32[8,2,4,512]{3,2,1,0:T(4,128)S(1)} %copy-done.3, f32[4,4,16,512]{3,2,1,0:T(8,128)S(1)} %copy-done.2), custom_call_target="tpu_custom_call" | custom-call | tf_op jit(solution)/shard_map/pallas_call | solution.py:419
  53.1 0.6 %constant_dynamic-slice_fusion = f32[3,128]{1,0:T(4,128)} fusion(f32[3,512]{1,0:T(4,128)S(1)} %get-tuple-element.5, s32[]{:T(128)S(6)} %select_n.3), kind=kLoop, calls=%fused_computation | loop fusion | bytes 3076 | tf_op jit(solution)/shard_map/dynamic_slice | solution.py:475
  53.7 0.8 %copy.11 = f32[2,2,4,16,512]{4,3,2,1,0:T(8,128)} copy(f32[2,2,4,16,512]{4,3,2,1,0:T(8,128)S(1)} %bitcast.4) | data formatting | bytes 1048576
Async XLA Ops:
  0.6 13.3 %copy-start.1 = (f32[240,1024]{1,0:T(8,128)S(1)}, f32[240,1024]{1,0:T(8,128)}, u32[]{:S(2)}) copy-start(f32[240,1024]{1,0:T(8,128)} %inc_hbm.1) | copy-start | bytes 2949124
  0.6 13.3 %copy-start.2 = (f32[4,4,16,512]{3,2,1,0:T(8,128)S(1)}, f32[4,4,16,512]{3,2,1,0:T(8,128)}, u32[]{:S(2)}) copy-start(f32[4,4,16,512]{3,2,1,0:T(8,128)} %constant.15.clone.azi_hbm) | copy-start | bytes 1572868
  0.7 13.3 %copy-start.3 = (f32[8,2,4,512]{3,2,1,0:T(4,128)S(1)}, f32[8,2,4,512]{3,2,1,0:T(4,128)}, u32[]{:S(2)}) copy-start(f32[8,2,4,512]{3,2,1,0:T(4,128)} %constant.14.clone.pol_hbm) | copy-start | bytes 393220
  0.7 13.3 %copy-start.4 = (f32[4,64]{1,0:T(4,128)S(1)}, f32[4,64]{1,0:T(4,128)}, u32[]{:S(2)}) copy-start(f32[4,64]{1,0:T(4,128)} %det.1) | copy-start | bytes 3076
  13.9 1.2 %copy-start = (f32[512,512]{1,0:T(8,128)S(1)}, f32[512,512]{1,0:T(8,128)}, u32[]{:S(2)}) copy-start(f32[512,512]{1,0:T(8,128)} %shard_map.95) | copy-start | bytes 3145732

commit v3 on v2

--- a/solution.py
+++ b/solution.py
@@ -58,59 +58,6 @@
     )
 
 
-def local_kernel(chunks, pos_ref, c_ref, z_ref, y_ref, x_ref, aw_ref, out_ref):
-    j = pl.program_id(0)
-    coef = c_ref.shape[1]
-    fields = c_ref.shape[2] // 2
-    width = fields // chunks
-
-    @pl.when(j == 0)
-    def _():
-        out_ref[...] = jnp.zeros_like(out_ref)
-
-    weight = aw_ref[...].T
-    lane = lax.broadcasted_iota(jnp.int32, weight.shape, 1)
-    column = jnp.sum(jnp.where(lane == j, weight, 0.0), axis=1, keepdims=True)
-    for h in range(chunks):
-        cols = slice(h * width, (h + 1) * width)
-        vr = c_ref[0, :, cols]
-        vi = c_ref[0, :, slice(fields + h * width, fields + (h + 1) * width)]
-        fr, fi = rotate(z_ref[0, 0], vr, vi)
-        fr, fi = rotate(y_ref[0, 0], fr.astype(jnp.bfloat16), fi.astype(jnp.bfloat16))
-        fr, fi = rotate(x_ref[0, 0], fr.astype(jnp.bfloat16), fi.astype(jnp.bfloat16))
-        out_ref[:coef, cols] += fr
-        out_ref[coef : 2 * coef, cols] += fi
-        wr, wi = vr.astype(jnp.float32), vi.astype(jnp.float32)
-        energy = (wr * wr + wi * wi) * column
-        out_ref[2 * coef : 2 * coef + 1, cols] += jnp.sum(energy, axis=0, keepdims=True)
-
-
-def local_part(coefficients, positions, shift_tables, absorb_weight, rows):
-    spheres, coef, columns = coefficients.shape
-    fields = columns // 2
-
-    def table(axis):
-        return pl.BlockSpec((1, 1, 2 * coef, coef), lambda j, pos: (axis, pos[axis, j], 0, 0))
-
-    return pl.pallas_call(
-        functools.partial(local_kernel, 1),
-        grid_spec=pltpu.PrefetchScalarGridSpec(
-            num_scalar_prefetch=1,
-            grid=(spheres,),
-            in_specs=[
-                pl.BlockSpec((1, coef, columns), lambda j, pos: (j, 0, 0)),
-                table(2),
-                table(1),
-                table(0),
-                pl.BlockSpec((spheres, coef), lambda j, pos: (0, 0)),
-            ],
-            out_specs=pl.BlockSpec(memory_space=pltpu.VMEM),
-        ),
-        out_shape=jax.ShapeDtypeStruct((rows, fields), jnp.float32),
-        compiler_params=pltpu.CompilerParams(dimension_semantics=("arbitrary",)),
-    )(positions.T, coefficients, shift_tables, shift_tables, shift_tables, absorb_weight)
-
-
 def split(value):
     high = value.astype(jnp.bfloat16)
     return high, (value - high.astype(jnp.float32)).astype(jnp.bfloat16)
@@ -118,9 +65,9 @@
 
 def far_kernel(
     sph_n, ang_n, coef, pol,
-    part, det, inc_hbm, pol_hbm, azi_hbm, amp_hbm, stats,
-    h_in, acc, in_a, in_b, in_z, gath, inc, tpol, tazi, basis, amp, pow_send, pow_recv,
-    s0, r0, sa, ra, sb, rb, sz, rz, ga, gb, gz, rg, s3, r3, s4, r4, lsem,
+    pos, absorb, det, coef_hbm, table_hbm, inc_hbm, pol_hbm, azi_hbm, amp_hbm, stats,
+    coefs, table_x, table_y, table_z, part,    h_in, acc, in_a, in_b, in_z, gath, inc, tpol, tazi, basis_high, basis_low, amp, pow_send, pow_recv,
+    s0, r0, sa, ra, sb, rb, sz, rz, ga, gb, gz, rg, s3, r3, s4, r4, lsem, csem, tsem,
 ):
     n = sph_n * ang_n
     q = ang_n // 2
@@ -146,6 +93,23 @@
     def device(d):
         return (d // ang_n, lax.rem(d, ang_n))
 
+    spheres = coefs.shape[0]
+    fields = coefs.shape[2] // 2
+
+    def coef_copy(j):
+        return pltpu.make_async_copy(coef_hbm.at[j], coefs.at[j], csem.at[j])
+
+    tables = (table_x, table_y, table_z)
+
+    def table_copy(axis):
+        return pltpu.make_async_copy(table_hbm.at[axis], tables[axis], tsem.at[axis])
+
+    table_copy(2).start()
+    coef_copy(0).start()
+    for j in range(1, spheres):
+        coef_copy(j).start()
+    table_copy(1).start()
+    table_copy(0).start()
     local = [
         pltpu.make_async_copy(inc_hbm, inc, lsem.at[0]),
         pltpu.make_async_copy(pol_hbm.at[sph], tpol, lsem.at[1]),
@@ -163,12 +127,51 @@
         return carry
 
     lax.fori_loop(1, n, greet, 0)
+    part[...] = jnp.zeros_like(part)
+    weight = absorb[...].T
+    lanes = lax.broadcasted_iota(jnp.int32, weight.shape, 1)
+
+    def step_first(j, carry):
+        coef_copy(j).wait()
+        vr, vi = coefs[j, :, :fields], coefs[j, :, fields:]
+        wr, wi = vr.astype(jnp.float32), vi.astype(jnp.float32)
+        column = jnp.sum(jnp.where(lanes == j, weight, 0.0), axis=1, keepdims=True)
+        energy = (wr * wr + wi * wi) * column
+        part[2 * coef : 2 * coef + 1, :] += jnp.sum(energy, axis=0, keepdims=True)
+        fr, fi = rotate(tables[2][pos[2, j]], vr, vi)
+        coefs[j, :, :fields] = fr.astype(jnp.bfloat16)
+        coefs[j, :, fields:] = fi.astype(jnp.bfloat16)
+        return carry
+
+    def step_second(j, carry):
+        fr, fi = rotate(tables[1][pos[1, j]], coefs[j, :, :fields], coefs[j, :, fields:])
+        coefs[j, :, :fields] = fr.astype(jnp.bfloat16)
+        coefs[j, :, fields:] = fi.astype(jnp.bfloat16)
+        return carry
+
+    def step_third(j, carry):
+        fr, fi = rotate(tables[0][pos[0, j]], coefs[j, :, :fields], coefs[j, :, fields:])
+        part[:coef, :] += fr
+        part[coef : 2 * coef, :] += fi
+        return carry
+
+    table_copy(2).wait()
+    lax.fori_loop(0, spheres, step_first, 0, unroll=2)
+    table_copy(1).wait()
+    lax.fori_loop(0, spheres, step_second, 0, unroll=4)
+    table_copy(0).wait()
+    lax.fori_loop(0, spheres, step_third, 0, unroll=4)
     pl.semaphore_wait(barrier, n - 1)
 
     remote = pltpu.make_async_remote_copy
 
+    r = gath.shape[1]
+
+    def piece_of(c):
+        return pl.ds(pl.multiple_of(c * r, 8), r)
+
     def copy0(c):
-        return remote(part.at[(1 - p) * m + c], h_in.at[c], s0.at[c], r0.at[c], partner, MESH)
+        return remote(part.at[piece_of((1 - p) * m + c)], h_in.at[c], s0.at[c], r0.at[c], partner, MESH)
 
     def send_a(a2, i, src):
         return remote(
@@ -209,7 +212,7 @@
 
     def copy4(d, slot):
         return pltpu.make_async_remote_copy(
-            pow_send, pow_recv.at[slot], s4.at[d], r4.at[slot], device(d), MESH
+            pow_send.at[lax.rem(d, ang_n)], pow_recv.at[slot], s4.at[d], r4.at[slot], device(d), MESH
         )
 
     def loop(low, high, body):
@@ -226,7 +229,7 @@
 
     def first(c):
         copy0(c).wait_recv()
-        acc[c] = part[p * m + c] + h_in[c]
+        acc[c] = part[piece_of(p * m + c), :] + h_in[c]
 
     for da in range(1, q):
         a2 = shift(a, da, q)
@@ -281,9 +284,10 @@
     block = pol * azi
     for cr in range(4):
         for i in range(pol):
-            basis[cr * block + i * azi : cr * block + (i + 1) * azi, :] = (
-                tpol[cr // 2, i : i + 1, :] * tazi[cr]
-            )
+            rows = slice(cr * block + i * azi, cr * block + (i + 1) * azi)
+            high, low = split(tpol[cr // 2, i : i + 1, :] * tazi[cr])
+            basis_high[rows, :] = high
+            basis_low[rows, :] = low
 
     def gather_sum(k, total):
         src = shift(z, k, nz)
@@ -332,12 +336,12 @@
     loop(0, m, lambda k: copy3(k, 1 - p).wait_recv())
 
     rows = gath.shape[0] * gath.shape[1]
-    fields = gath.shape[2]
     anchor = gath[...].reshape(rows, fields)
     a_high, a_low = split(anchor[: 2 * coef])
-    w_high, w_low = split(basis[:, : 2 * coef])
+    w_high, w_low = basis_high[:, : 2 * coef], basis_low[:, : 2 * coef]
     dot = functools.partial(jnp.dot, preferred_element_type=jnp.float32)
-    far = dot(w_high, a_high) + (dot(w_high, a_low) + dot(w_low, a_high))
+    both = dot(jnp.concatenate([w_high, w_low], 0), a_high)
+    far = both[: 4 * block] + (dot(w_high, a_low) + both[4 * block :])
     amp[...] = far
     out_copy = pltpu.make_async_copy(amp, amp_hbm, lsem.at[0])
     out_copy.start()
@@ -355,15 +359,24 @@
             piece = far[cr * block + i * azi : cr * block + (i + 1) * azi, :]
             total = total + piece * piece
         power = power + jnp.sum(total * weight, axis=0, keepdims=True)
-    pow_send[...] = power
-    pow_recv[me] = power
+    share = fields // ang_n
+
+    def own(row):
+        value = row[:, :share]
+        for g in range(1, ang_n):
+            value = jnp.where(ang == g, row[:, g * share : (g + 1) * share], value)
+        return value
+
+    for g in range(ang_n):
+        pow_send[g] = power[:, g * share : (g + 1) * share]
+    pow_recv[me] = own(power)
     loop(1, n, lambda k: copy4(lax.rem(me + k, n), me).start())
 
-    stats[0:1, :] = jnp.sum(
+    stats[0:1, :] = own(jnp.sum(
         inc[:, :fields] * anchor[:coef] + inc[:, fields:] * anchor[coef : 2 * coef],
         axis=0, keepdims=True,
-    )
-    stats[1:2, :] = anchor[2 * coef : 2 * coef + 1]
+    ))
+    stats[1:2, :] = own(anchor[2 * coef : 2 * coef + 1])
 
     def finish(k):
         copy0(k).wait_send()
@@ -403,28 +416,36 @@
     out_copy.wait()
 
 
-def far_part(part, detector, incident, polar, azim, sph_n, ang_n):
-    n, r, fields = part.shape
+def far_part(positions, absorb_weight, detector, coefficients, shift_tables, incident, polar, azim, sph_n, ang_n):
+    n = sph_n * ang_n
+    spheres, coef, columns = coefficients.shape
+    fields = columns // 2
+    r = 8 * -(-(2 * coef + 1) // (8 * n))
     m = n // 2
     nz = sph_n // (ang_n // 2)
     line = n // ang_n
-    coef = incident.shape[0]
     pol = detector.shape[0]
     azi = azim.shape[2]
     wide = polar.shape[3]
+    smem = pl.BlockSpec(memory_space=pltpu.SMEM)
     vmem = pl.BlockSpec(memory_space=pltpu.VMEM)
-    hbm = pl.BlockSpec(memory_space=pl.ANY)
+    hbm = pl.BlockSpec(memory_space=pltpu.HBM)
     f32 = jnp.float32
     dma = pltpu.SemaphoreType.DMA
     return pl.pallas_call(
         functools.partial(far_kernel, sph_n, ang_n, coef, pol),
         out_shape=(
             jax.ShapeDtypeStruct((4 * pol * azi, fields), f32),
-            jax.ShapeDtypeStruct((3, fields), f32),
+            jax.ShapeDtypeStruct((3, fields // ang_n), f32),
         ),
-        in_specs=[vmem, vmem, hbm, hbm, hbm],
-        out_specs=(hbm, vmem),
+        in_specs=[smem, vmem, vmem, hbm, hbm, hbm, hbm, hbm],
+        out_specs=(pl.BlockSpec(memory_space=pl.ANY), vmem),
         scratch_shapes=[
+            pltpu.VMEM(coefficients.shape, jnp.bfloat16),
+            pltpu.VMEM(shift_tables.shape[1:], jnp.bfloat16),
+            pltpu.VMEM(shift_tables.shape[1:], jnp.bfloat16),
+            pltpu.VMEM(shift_tables.shape[1:], jnp.bfloat16),
+            pltpu.VMEM((n * r, fields), f32),
             pltpu.VMEM((m, r, fields), f32),
             pltpu.VMEM((m, r, fields), f32),
             pltpu.VMEM((m, r, fields), f32),
@@ -434,25 +455,24 @@
             pltpu.VMEM(incident.shape, f32),
             pltpu.VMEM((2, pol, wide), f32),
             pltpu.VMEM((4, azi, wide), f32),
-            pltpu.VMEM((4 * pol * azi, wide), f32),
+            pltpu.VMEM((4 * pol * azi, wide), jnp.bfloat16),
+            pltpu.VMEM((4 * pol * azi, wide), jnp.bfloat16),
             pltpu.VMEM((4 * pol * azi, fields), f32),
-            pltpu.VMEM((1, fields), f32),
-            pltpu.VMEM((n, 1, fields), f32),
+            pltpu.VMEM((ang_n, 1, fields // ang_n), f32),
+            pltpu.VMEM((n, 1, fields // ang_n), f32),
         ]
         + [dma((size,)) for size in (m, m, m, m, line, line, nz, nz, m, line, nz, m, m, m)]
         + [dma((n,))] * 2
-        + [dma((3,))],
+        + [dma((3,)), dma((spheres,)), dma((3,))],
         compiler_params=pltpu.CompilerParams(
-            collective_id=0, has_side_effects=True, vmem_limit_bytes=48 * 2**20
+            collective_id=0, has_side_effects=True, vmem_limit_bytes=60 * 2**20
         ),
-    )(part, detector, incident, polar, azim)
+    )(positions.T, absorb_weight, detector, coefficients, shift_tables, incident, polar, azim)
 
 
 def shards(sph_n, ang_n, coefficients, positions, shift_tables, absorb_weight, incident, detector):
     fields = coefficients.shape[2] // 2
     coef = coefficients.shape[1]
-    n = sph_n * ang_n
-    chunk = 8 * -(-(2 * coef + 1) // (8 * n))
     pol, azim_total = detector.shape
     polar_total = pol * sph_n
     azi = azim_total // ang_n
@@ -466,14 +486,11 @@
     table_azim = np.zeros((ang_n, 4, azi, wide), np.float32)
     table_azim[..., : 2 * coef] = azim.reshape(4, ang_n, azi, 2 * coef).transpose(1, 0, 2, 3)
 
-    part = local_part(coefficients, positions, shift_tables, absorb_weight, n * chunk)
     amplitude, stats = far_part(
-        part.reshape(n, chunk, fields), detector, incident,
+        positions, absorb_weight, detector, coefficients, shift_tables, incident,
         jnp.asarray(table_polar), jnp.asarray(table_azim), sph_n, ang_n,
     )
-    share = fields // ang_n
-    own = lax.dynamic_slice_in_dim(stats, lax.axis_index("ang") * share, share, 1)
-    return (amplitude.reshape(2, 2, pol, azi, fields), own)
+    return (amplitude.reshape(2, 2, pol, azi, fields), stats)
 
 
 def solution(mesh):

time: 54.8 us -> 50.4 us (0.920)
  Pallas kernels: 51.2 us -> 46.4 us
    pallas_call x1 -> x0, Pallas kernels: 13.2 us -> none  [local_part(): pl.pallas_call(functools.partial(local_kernel, 1), grid_spec=pltpu.Prefet...]
    pallas_call x1, Pallas kernels: 37.9 us -> 46.4 us  [far_part(): pl.pallas_call(functools.partial(far_kernel, sph_n, ang_n, coef, pol), ou...]
    unnamed x11 -> x2, local copies, waits for them, and re-layouts: 2.03 us -> 3.13 us
    dynamic_slice x1 -> x0, local copies, waits for them, and re-layouts: 0.59 us -> none  [shards(): lax.dynamic_slice_in_dim(stats, lax.axis_index('ang') * share, share, 1)]
where the time goes in v3:
time: 50.4 us; the launch traced here: 50.2 us
  Pallas kernels  46.4 us (92%)
  local copies, waits for them, and re-layouts  3.13 us (6%)
  between operations  0.64 us (1%)
    pallas_call x1, Pallas kernels, far_part(): pl.pallas_call(functools.partial(far_kernel, sph_n, ang_n, coef, pol), ou...  46.4 us
    unnamed x2, local copies, waits for them, and re-layouts  3.13 us

profile of v3, /device:TPU:0, one launch (start us, length us, event | category | flops | bytes accessed | tf_op | source)
XLA Modules:
  0.0 50.2 jit_solution(8003597233532494414)
XLA Ops:
  0.6 46.4 %shard_map.95 = (f32[256,512]{1,0:T(8,128)}, f32[3,128]{1,0:T(4,128)}) custom-call(s32[3,8]{1,0:T(4,128)} %bitcast.3, f32[8,240]{1,0:T(8,128)} %absorb.1, f32[4,64]{1,0:T(4,128)} %det.1, bf16[8,240,1024]{2,1,0:T(8,128)(2,1)} %coef_hbm.1, bf16[3,8,480,240]{3,2,1,0:T(8,128)(2,1)} %table_hbm.1, f32[240,1024]{1,0:T(8,128)} %inc_hbm.1, ...), custom_call_target="tpu_custom_call" | custom-call | tf_op jit(solution)/shard_map/pallas_call | solution.py:435
  47.1 1.9 %copy.12 = f32[2,2,4,16,512]{4,3,2,1,0:T(8,128)} copy(f32[2,2,4,16,512]{4,3,2,1,0:T(8,128)} %bitcast.2) | data formatting | bytes 1048576
  49.0 1.3 %copy.13 = f32[3,128]{1,0:T(4,128)} copy(f32[3,128]{1,0:T(4,128)} %get-tuple-element.9) | data formatting | bytes 3072
